TPU v7x, 256 devices: a whole 4x4x8 slice. The times are simulated.
256 devices in a mesh: prow: 16 (over y_hi, z), pcol: 16 (over x, y_lo, core).
Axes of the slice: x: 4, y: 4 (y_hi: 2, y_lo: 2; y = y_hi * 2 + y_lo), z: 8, core: 2. Of those that a mesh axis runs over, the one named last changes fastest.
Arguments:
- ainv: float32 [20480, 20480], P('prow', 'pcol'), may hold values from -0.15625 to 0.15625
- panels: float32 [3, 20480, 512], P(None, ('prow', 'pcol')), may hold values from -0.8 to 0.8
- ancestors: int32 [3, 2560], P(None, ('prow', 'pcol')), may hold values from 0 to 1, as said below
- dinv: float32 [3, 512, 512], P(None, 'prow', 'pcol'), may hold values from -6 to 6
Outputs:
- u_panel: float32 [3, 20480, 512], P(None, ('prow', 'pcol'))
- diag: float32 [3, 512, 512], P(None, 'prow', 'pcol')
Inputs may be any that keep to these rules, and one draw needn't show every extreme that they name: `ancestors`: each entry is 0 or 1; the share of ancestor blocks varies strongly between regions of the rows.
All inputs are finite; a program needn't handle non-finite values.
Results may differ from a plain program's by a relative error of at most 0.00007.
Values sent between devices are 32-bit elements; how exact they have to be, the bound alone decides.
A program may use at most 128 MiB of HBM per device.

v0:
```python
import jax
import jax.numpy as jnp
from jax import lax
from jax.sharding import Mesh
from jax.sharding import PartitionSpec as P

S = 512
NSUP = 3
BLK = 8
PCOL = ("pcol_0", "pcol_1", "pcol_2")
PROW_PCOL = ("prow", "pcol_0", "pcol_1", "pcol_2")


def split_up(value, dim, peers):
    before, after = (value.shape[:dim], value.shape[dim + 1 :])
    return jnp.moveaxis(value.reshape(*before, peers, -1, *after), dim, 0)


def sum_by_chip(value, chips, core, dim):
    sizes = (lax.axis_size(chips), lax.axis_size(core))
    tiles = split_up(value, dim, sizes[0] * sizes[1])
    inside = tiles.shape[1:]
    tiles = tiles.reshape(*sizes, *inside).swapaxes(0, 1).reshape(-1, *inside)
    tiles = lax.psum_scatter(tiles, core, scatter_dimension=0, tiled=True)
    return lax.psum_scatter(tiles, chips, scatter_dimension=0, tiled=True)[0]


def sent_and_summed(value, axis, dim):
    peers = lax.axis_size(axis)
    tiles = lax.all_to_all(split_up(value, dim, peers), axis, 0, 0, tiled=True)
    return jnp.sum(tiles, axis=0)


def apply_rows(columns, piece):

    def dense_product():
        return jnp.dot(columns, piece, precision=lax.Precision.HIGHEST)

    def no_product():
        return jnp.zeros((columns.shape[0], piece.shape[1]), jnp.float32)

    return lax.cond(jnp.any(piece != 0.0), dense_product, no_product)


def on_device(ainv, panels, ancestors, dinv):
    row_flags = jnp.repeat(ancestors, BLK, axis=1).astype(jnp.float32)
    masked = panels * row_flags[:, :, None]
    local_rows = ainv.shape[0]
    empty = jnp.zeros((NSUP, local_rows, S), jnp.float32)
    total = empty
    piece = lax.all_gather(masked, "prow", axis=1, tiled=True)
    for member in range(NSUP):
        total = total.at[member].add(apply_rows(ainv, piece[member]))
    partial_value = sum_by_chip(total, ("pcol_0", "pcol_1"), "pcol_2", 1)
    u_panel = -(row_flags[:, :, None] * partial_value)
    local_terms = jnp.einsum("srn,srm->snm", masked, u_panel, precision=lax.Precision.HIGHEST)
    by_columns = sent_and_summed(local_terms, PCOL, 2)
    own_block = sent_and_summed(by_columns, "prow", 1)
    diag = dinv - own_block
    return (u_panel, diag)


def solution(mesh):
    split = Mesh(
        mesh.devices.reshape(mesh.shape["prow"], 4, 2, 2), ("prow", "pcol_0", "pcol_1", "pcol_2")
    )
    in_specs = (
        P("prow", PCOL),
        P(None, PROW_PCOL, None),
        P(None, PROW_PCOL),
        P(None, "prow", PCOL),
    )
    out_specs = (P(None, PROW_PCOL, None), P(None, "prow", PCOL))
    return jax.shard_map(
        on_device, mesh=split, in_specs=in_specs, out_specs=out_specs, check_vma=False
    )
```

profile of v0, /device:TPU:32, one launch (start us, length us, event | category | flops | bytes accessed | tf_op | source)
XLA Modules:
  0.0 404.4 jit_solution(11009436670930716270)
XLA Ops:
  7.2 0.0 all-gather.2.cloned.1.call-start
  7.2 0.7 convert_element_type.20
  7.9 0.1 broadcast_in_dim.2
  8.0 0.1 convert_element_type.21
  8.1 1.9 broadcast_multiply_fusion
  10.0 0.0 all-gather.2.cloned.1.call-update
  10.0 0.0 reduce-scatter.3.cloned.1.call-start
  10.0 132.6 %all-gather.2.cloned.1.call-done = f32[3,1280,512]{2,1,0:T(8,128)} async-done(((f32[3,80,512]{2,1,0:T(8,128)}), f32[3,1280,512]{2,1,0:T(8,128)}) %all-gather.2.cloned.1.call-update) | async-done | bytes 7864336 | tf_op jit(solution)/shard_map/all_gather | solution.py:51
  142.6 5.0 %compare_reduce_fusion = (pred[]{:T(512)}, pred[]{:T(512)}, pred[]{:T(512)}) fusion(f32[3,1280,512]{2,1,0:T(8,128)} %all-gather.2.cloned.1.call-done), kind=kLoop, calls=%fused_computation.9 | loop fusion | flops 3932157 | bytes 7864323 | tf_op jit(solution)/shard_map/reduce_or | solution.py:42
  149.6 6.7 %slice_bitcast_fusion = (f32[1280,512]{1,0:T(8,128)}, f32[1280,512]{1,0:T(8,128)}, f32[1280,512]{1,0:T(8,128)}) fusion(f32[3,1280,512]{2,1,0:T(8,128)} %all-gather.2.cloned.1.call-done), kind=kLoop, calls=%fused_computation.4 | loop fusion | bytes 15728640 | tf_op jit(solution)/shard_map/squeeze | solution.py:53
  156.2 13.4 %conditional.4 = (f32[1,1280,512]{2,1,0:T(8,128)S(1)}) conditional(s32[]{:T(128)} %convert_element_type.23, () %tuple.46, (f32[1280,1280]{1,0:T(8,128)}, f32[1280,512]{1,0:T(8,128)}) %tuple.47), branch_computations={%region_4.0_spmd, %region_5.0_spmd} | conditional | flops 10066329600 | bytes 11796488 | solution.py:42
  156.2 13.4 %convolution_bitcast_fusion.1 = f32[1,1280,512]{2,1,0:T(8,128)S(1)} fusion(f32[1280,1280]{1,0:T(8,128)} %get-tuple-element.62, f32[1280,512]{1,0:T(8,128)} %get-tuple-element.63), kind=kOutput, calls=%fused_computation.1 | convolution fusion | flops 10066329600 | bytes 11796480 | tf_op jit(solution)/shard_map/cond/branch_1_fun/dot_general | solution.py:37
  169.6 17.6 %conditional.3 = (f32[3,1280,512]{2,1,0:T(8,128)}) conditional(s32[]{:T(128)} %convert_element_type.22, () %tuple.44, (f32[1280,1280]{1,0:T(8,128)}, f32[1280,512]{1,0:T(8,128)}) %tuple.45), branch_computations={%region_1.0_spmd, %region_2.0_spmd} | conditional | flops 10066329600 | bytes 22282252 | solution.py:42
  169.8 13.4 %convolution_bitcast_fusion = f32[1,1280,512]{2,1,0:T(8,128)S(1)} fusion(f32[1280,1280]{1,0:T(8,128)} %get-tuple-element.60, f32[1280,512]{1,0:T(8,128)} %get-tuple-element.61), kind=kOutput, calls=%fused_computation | convolution fusion | flops 10066329600 | bytes 11796480 | tf_op jit(solution)/shard_map/cond/branch_1_fun/dot_general | solution.py:37
  183.3 4.0 scatter-add.9
  187.3 1.8 constant_dynamic-update-slice_fusion
  189.0 13.4 %conditional.5 = (f32[1,1280,512]{2,1,0:T(8,128)S(1)}) conditional(s32[]{:T(128)} %convert_element_type.24, () %tuple.48, (f32[1280,1280]{1,0:T(8,128)}, f32[1280,512]{1,0:T(8,128)}) %tuple.49), branch_computations={%region_7.0_spmd, %region_8.0_spmd} | conditional | flops 10066329600 | bytes 11796488 | solution.py:42
  189.0 13.4 %convolution_bitcast_fusion.2 = f32[1,1280,512]{2,1,0:T(8,128)S(1)} fusion(f32[1280,1280]{1,0:T(8,128)} %get-tuple-element.64, f32[1280,512]{1,0:T(8,128)} %get-tuple-element.65), kind=kOutput, calls=%fused_computation.2 | convolution fusion | flops 10066329600 | bytes 11796480 | tf_op jit(solution)/shard_map/cond/branch_1_fun/dot_general | solution.py:37
  202.4 3.9 fusion
  206.3 8.0 %copy.9 = f32[2,8,3,80,512]{4,3,2,1,0:T(8,128)} copy(f32[2,8,3,80,512]{4,3,0,1,2:T(8,128)} %bitcast.45) | data formatting | bytes 15728640 | tf_op jit(solution)/shard_map/transpose | solution.py:23
  214.3 0.0 reduce-scatter.3.cloned.1.call-update
  214.3 0.0 copy-start
  214.3 0.3 reduce-scatter.5.cloned.1.call-start
  214.6 20.3 %reduce-scatter.3.cloned.1.call-done = f32[8,3,80,512]{3,2,1,0:T(8,128)} async-done(((f32[16,3,80,512]{3,2,1,0:T(8,128)}), f32[8,3,80,512]{3,2,1,0:T(8,128)}) %reduce-scatter.3.cloned.1.call-update) | async-done | bytes 3932176 | tf_op jit(solution)/shard_map/reduce_scatter | solution.py:24
  234.9 0.0 reduce-scatter.5.cloned.1.call-update
  235.0 91.7 %reduce-scatter.5.cloned.1.call-done = f32[1,3,80,512]{3,2,1,0:T(8,128)} async-done(((f32[8,3,80,512]{3,2,1,0:T(8,128)}), f32[1,3,80,512]{3,2,1,0:T(8,128)}) %reduce-scatter.5.cloned.1.call-update) | async-done | bytes 491536 | tf_op jit(solution)/shard_map/reduce_scatter | solution.py:25
  326.7 1.1 fusion.1
  327.8 0.0 copy-done
  327.8 0.0 copy-start.1
  327.9 2.7 fusion.2
  330.6 0.0 copy-done.1
  330.6 0.5 copy.16
  331.1 43.8 %all_to_all.10 = f32[16,3,512,32]{2,3,1,0:T(8,128)S(1)} all-to-all(f32[16,3,512,32]{2,3,1,0:T(8,128)S(1)} %bitcast.48), channel_id=1, replica_groups=mesh['prow'=16,'pcol_0'=4,'pcol_1'=2,'pcol_2'=2] {'pcol_0','pcol_1','pco..., dimensions={0} | all-to-all | bytes 6291456 | tf_op jit(solution)/shard_map/all_to_all | solution.py:30
  374.9 0.3 reduce_sum.18
  375.2 0.2 reshape.129
  375.4 0.0 copy-start.2
  375.4 0.4 copy.12
  375.8 0.3 reshape.130
  376.2 19.1 %all_to_all.11 = f32[16,1,3072]{2,1,0:T(1,128)S(1)} all-to-all(f32[16,1,3072]{2,1,0:T(1,128)S(1)} %reshape.130), channel_id=1, replica_groups=mesh['prow'=16,'pcol_0'=4,'pcol_1'=2,'pcol_2'=2] {'prow'}, dimensions={0} | all-to-all | bytes 393216 | tf_op jit(solution)/shard_map/all_to_all | solution.py:30
  395.3 0.5 broadcast.77
  395.8 1.1 reduce.6
  396.9 0.2 reshape.131
  397.1 0.1 reduce_sum.19
  397.2 0.0 copy-done.2
  397.2 0.6 sub.3
Async XLA Ops:
  7.2 135.5 %all-gather.2.cloned.1.call-start = ((), (), s32[]{:S(2)}) async-start(), calls=%async_computation.4 | async-start | bytes 8355840 | tf_op jit(solution)/shard_map/all_gather | solution.py:51
  10.0 224.9 %reduce-scatter.3.cloned.1.call-start = ((), (), s32[]{:S(2)}) async-start(), calls=%async_computation.5 | async-start | bytes 11796480 | tf_op jit(solution)/shard_map/reduce_scatter | solution.py:24
  214.3 113.5 %copy-start = (f32[3,80,512]{2,1,0:T(8,128)S(1)}, f32[3,80,512]{2,1,0:T(8,128)}, u32[]{:S(2)}) copy-start(f32[3,80,512]{2,1,0:T(8,128)} %broadcast_multiply_fusion) | copy-start | bytes 1474564
  214.3 112.4 %reduce-scatter.5.cloned.1.call-start = ((), (), s32[]{:S(2)}) async-start(), calls=%async_computation.6 | async-start | bytes 4423680 | tf_op jit(solution)/shard_map/reduce_scatter | solution.py:25
  327.8 2.7 copy-start.1
  375.4 21.8 %copy-start.2 = (f32[3,32,32]{2,1,0:T(8,128)S(1)}, f32[3,32,32]{2,1,0:T(8,128)}, u32[]{:S(2)}) copy-start(f32[3,32,32]{2,1,0:T(8,128)} %param.19) | copy-start | bytes 36868
Sparse Core Ops, SparseCore 0:
  11.1 131.4 all-gather.1
  214.5 20.4 reduce-scatter.2
  237.5 89.1 reduce-scatter.4
where the time goes:
time: 405 us; the launch traced here: 404 us
  waiting for transfers between devices  245 us (60%)
  blocking collectives  62.9 us (16%)
  matrix products  42.9 us (11%)
  local copies, waits for them, and re-layouts  22.8 us (6%)
  between operations  15.8 us (4%)
  other arithmetic  14.7 us (4%)
    all_gather x1, waiting for transfers between devices, on_device(): piece = lax.all_gather(masked, 'prow', axis=1, tiled=True)  133 us
    reduce_scatter x1, waiting for transfers between devices, sum_by_chip(): return lax.psum_scatter(tiles, chips, scatter_dimension=0, tiled=True)[0]  91.7 us
    all_to_all x2, blocking collectives, sent_and_summed(): tiles = lax.all_to_all(split_up(value, dim, peers), axis, 0, 0, tiled=True)  62.9 us
    dot_general x3, matrix products, dense_product(): return jnp.dot(columns, piece, precision=lax.Precision.HIGHEST)  40.2 us
    reduce_scatter x1, waiting for transfers between devices, sum_by_chip(): tiles = lax.psum_scatter(tiles, core, scatter_dimension=0, tiled=True)  20.3 us
  transfers between devices with their start and end apart: 3, of which 3 were waited for; matrix products, arithmetic and copies ran while one was open for 0% of the time, Pallas kernels for 0%

commit v1 on v0

--- a/solution.py
+++ b/solution.py
@@ -48,7 +48,15 @@
     local_rows = ainv.shape[0]
     empty = jnp.zeros((NSUP, local_rows, S), jnp.float32)
     total = empty
-    piece = lax.all_gather(masked, "prow", axis=1, tiled=True)
+    piece = jnp.concatenate(
+        lax.all_to_all(
+            jnp.stack(lax.axis_size("prow") * [masked]),
+            axis_name="prow",
+            split_axis=0,
+            concat_axis=0,
+        ),
+        axis=1,
+    )
     for member in range(NSUP):
         total = total.at[member].add(apply_rows(ainv, piece[member]))
     partial_value = sum_by_chip(total, ("pcol_0", "pcol_1"), "pcol_2", 1)

time: 405 us -> 471 us (1.16)
  waiting for transfers between devices: 245 us -> 296 us
  starting transfers between devices: 0.34 us -> 11.5 us
    all_to_all x0 -> x1, waiting for transfers between devices: none -> 177 us  [on_device(): lax.all_to_all(jnp.stack(lax.axis_size('prow') * [masked]), axis_name='pr...]
    all_gather x1 -> x0, waiting for transfers between devices: 133 us -> none  [on_device(): piece = lax.all_gather(masked, 'prow', axis=1, tiled=True)]
    all_to_all x0 -> x1, starting transfers between devices: none -> 11.2 us  [on_device(): lax.all_to_all(jnp.stack(lax.axis_size('prow') * [masked]), axis_name='pr...]
    slice x0 -> x1, local copies, waits for them, and re-layouts: none -> 6.8 us  [on_device(): total = total.at[member].add(apply_rows(ainv, piece[member]))]
    reduce_scatter x1, waiting for transfers between devices: 20.3 us -> 27 us  [sum_by_chip(): tiles = lax.psum_scatter(tiles, core, scatter_dimension=0, tiled=True)]
    squeeze x1 -> x0, local copies, waits for them, and re-layouts: 6.65 us -> none  [on_device(): total = total.at[member].add(apply_rows(ainv, piece[member]))]
where the time goes in v1:
time: 471 us; the launch traced here: 470 us
  waiting for transfers between devices  296 us (63%)
  blocking collectives  62.9 us (13%)
  matrix products  42.9 us (9%)
  local copies, waits for them, and re-layouts  27.1 us (6%)
  between operations  16.1 us (3%)
  other arithmetic  13.9 us (3%)
  starting transfers between devices  11.5 us (2%)
    all_to_all x1, waiting for transfers between devices, on_device(): lax.all_to_all(jnp.stack(lax.axis_size('prow') * [masked]), axis_name='pr...  177 us
    reduce_scatter x1, waiting for transfers between devices, sum_by_chip(): return lax.psum_scatter(tiles, chips, scatter_dimension=0, tiled=True)[0]  91.8 us
    all_to_all x2, blocking collectives, sent_and_summed(): tiles = lax.all_to_all(split_up(value, dim, peers), axis, 0, 0, tiled=True)  62.9 us
    dot_general x3, matrix products, dense_product(): return jnp.dot(columns, piece, precision=lax.Precision.HIGHEST)  40.3 us
    reduce_scatter x1, waiting for transfers between devices, sum_by_chip(): tiles = lax.psum_scatter(tiles, core, scatter_dimension=0, tiled=True)  27 us
    all_to_all x1, starting transfers between devices, on_device(): lax.all_to_all(jnp.stack(lax.axis_size('prow') * [masked]), axis_name='pr...  11.2 us
  transfers between devices with their start and end apart: 3, of which 3 were waited for; matrix products, arithmetic and copies ran while one was open for 0% of the time, Pallas kernels for 0%

profile of v1, /device:TPU:32, one launch (start us, length us, event | category | flops | bytes accessed | tf_op | source)
XLA Modules:
  0.0 470.4 jit_solution(3059026423331615971)
XLA Ops:
  7.2 0.7 convert_element_type.20
  7.8 0.1 broadcast_in_dim.2
  7.9 0.1 convert_element_type.21
  8.0 1.1 broadcast_multiply_fusion
  9.1 4.2 stack.2
  13.3 11.2 %all-to-all-start = ((f32[16,3,80,512]{3,2,1,0:T(8,128)}), f32[16,3,80,512]{3,2,1,0:T(8,128)}, u32[]{:S(2)}, u32[]{:S(2)}) async-start(f32[16,3,80,512]{3,2,1,0:T(8,128)} %stack.2), calls=%async_computation | async-start | bytes 15728640 | tf_op jit(solution)/shard_map/all_to_all | solution.py:52
  24.5 0.0 reduce-scatter.3.cloned.1.call-start
  24.6 176.9 %all-to-all-done = f32[16,3,80,512]{3,2,1,0:T(8,128)} async-done(((f32[16,3,80,512]{3,2,1,0:T(8,128)}), f32[16,3,80,512]{3,2,1,0:T(8,128)}, u32[]{:S(2)}, u32[]{:S(2)}) %all-to-all-start) | async-done | bytes 7864352 | tf_op jit(solution)/shard_map/all_to_all | solution.py:52
  201.5 5.1 %compare_reduce_fusion = (pred[]{:T(512)}, pred[]{:T(512)}, pred[]{:T(512)}) fusion(f32[3,16,80,512]{3,2,0,1:T(8,128)} %bitcast.9), kind=kLoop, calls=%fused_computation.6 | loop fusion | flops 3932157 | bytes 7864323 | tf_op jit(solution)/shard_map/reduce_or | solution.py:42
  206.5 6.8 %fusion.2 = (f32[1,16,80,512]{3,2,0,1:T(8,128)}, f32[1,16,80,512]{3,2,0,1:T(8,128)}, f32[1,16,80,512]{3,2,0,1:T(8,128)}) fusion(f32[3,16,80,512]{3,2,0,1:T(8,128)} %bitcast.9), kind=kLoop, calls=%fused_computation.13 | loop fusion | bytes 15728640 | tf_op jit(solution)/shard_map/slice | solution.py:61
  215.3 13.4 %conditional.4 = (f32[1,1280,512]{2,1,0:T(8,128)S(1)}) conditional(s32[]{:T(128)} %convert_element_type.23, () %tuple.46, (f32[1280,1280]{1,0:T(8,128)}, f32[1,16,80,512]{3,2,0,1:T(8,128)}) %tuple.47), branch_computations={%region_4.0_spmd, %region_5.0_spmd} | conditional | flops 10066329600 | bytes 11796488 | solution.py:42
  215.3 13.4 %convolution_bitcast_fusion.1 = f32[1,1280,512]{2,1,0:T(8,128)S(1)} fusion(f32[1280,1280]{1,0:T(8,128)} %get-tuple-element.62, f32[1280,512]{1,0:T(8,128)} %bitcast.50), kind=kOutput, calls=%fused_computation.1 | convolution fusion | flops 10066329600 | bytes 11796480 | tf_op jit(solution)/shard_map/cond/branch_1_fun/dot_general | solution.py:37
  228.7 17.7 %conditional.3 = (f32[3,1280,512]{2,1,0:T(8,128)}) conditional(s32[]{:T(128)} %convert_element_type.22, () %tuple.44, (f32[1280,1280]{1,0:T(8,128)}, f32[1,16,80,512]{3,2,0,1:T(8,128)}) %tuple.45), branch_computations={%region_1.0_spmd, %region_2.0_spmd} | conditional | flops 10066329600 | bytes 22282252 | solution.py:42
  228.9 13.4 %convolution_bitcast_fusion = f32[1,1280,512]{2,1,0:T(8,128)S(1)} fusion(f32[1280,1280]{1,0:T(8,128)} %get-tuple-element.60, f32[1280,512]{1,0:T(8,128)} %bitcast.49), kind=kOutput, calls=%fused_computation | convolution fusion | flops 10066329600 | bytes 11796480 | tf_op jit(solution)/shard_map/cond/branch_1_fun/dot_general | solution.py:37
  242.4 4.1 scatter-add.9
  246.5 1.8 constant_dynamic-update-slice_fusion
  248.2 13.4 %conditional.5 = (f32[1,1280,512]{2,1,0:T(8,128)S(1)}) conditional(s32[]{:T(128)} %convert_element_type.24, () %tuple.48, (f32[1280,1280]{1,0:T(8,128)}, f32[1,16,80,512]{3,2,0,1:T(8,128)}) %tuple.49), branch_computations={%region_7.0_spmd, %region_8.0_spmd} | conditional | flops 10066329600 | bytes 11796488 | solution.py:42
  248.2 13.4 %convolution_bitcast_fusion.2 = f32[1,1280,512]{2,1,0:T(8,128)S(1)} fusion(f32[1280,1280]{1,0:T(8,128)} %get-tuple-element.64, f32[1280,512]{1,0:T(8,128)} %bitcast.48), kind=kOutput, calls=%fused_computation.2 | convolution fusion | flops 10066329600 | bytes 11796480 | tf_op jit(solution)/shard_map/cond/branch_1_fun/dot_general | solution.py:37
  261.6 3.8 fusion
  265.4 7.9 %copy.12 = f32[2,8,3,80,512]{4,3,2,1,0:T(8,128)} copy(f32[2,8,3,80,512]{4,3,0,1,2:T(8,128)} %bitcast.43) | data formatting | bytes 15728640 | tf_op jit(solution)/shard_map/transpose | solution.py:23
  273.4 0.0 reduce-scatter.3.cloned.1.call-update
  273.4 0.3 reduce-scatter.5.cloned.1.call-start
  273.7 27.0 %reduce-scatter.3.cloned.1.call-done = f32[8,3,80,512]{3,2,1,0:T(8,128)} async-done(((f32[16,3,80,512]{3,2,1,0:T(8,128)}), f32[8,3,80,512]{3,2,1,0:T(8,128)}) %reduce-scatter.3.cloned.1.call-update) | async-done | bytes 3932176 | tf_op jit(solution)/shard_map/reduce_scatter | solution.py:24
  300.7 0.0 reduce-scatter.5.cloned.1.call-update
  300.7 91.8 %reduce-scatter.5.cloned.1.call-done = f32[1,3,80,512]{3,2,1,0:T(8,128)} async-done(((f32[8,3,80,512]{3,2,1,0:T(8,128)}), f32[1,3,80,512]{3,2,1,0:T(8,128)}) %reduce-scatter.5.cloned.1.call-update) | async-done | bytes 491536 | tf_op jit(solution)/shard_map/reduce_scatter | solution.py:25
  392.5 1.1 fusion.1
  393.6 0.0 copy-start
  393.6 2.7 fusion.3
  396.3 0.0 copy-done
  396.3 0.5 copy.19
  396.9 43.8 %all_to_all.15 = f32[16,3,512,32]{2,3,1,0:T(8,128)S(1)} all-to-all(f32[16,3,512,32]{2,3,1,0:T(8,128)S(1)} %bitcast.46), channel_id=1, replica_groups=mesh['prow'=16,'pcol_0'=4,'pcol_1'=2,'pcol_2'=2] {'pcol_0','pcol_1','pco..., dimensions={0} | all-to-all | bytes 6291456 | tf_op jit(solution)/shard_map/all_to_all | solution.py:30
  440.7 0.3 reduce_sum.18
  441.0 0.2 reshape.142
  441.2 0.0 copy-start.1
  441.2 0.4 copy.15
  441.6 0.3 reshape.143
  441.9 19.1 %all_to_all.16 = f32[16,1,3072]{2,1,0:T(1,128)S(1)} all-to-all(f32[16,1,3072]{2,1,0:T(1,128)S(1)} %reshape.143), channel_id=1, replica_groups=mesh['prow'=16,'pcol_0'=4,'pcol_1'=2,'pcol_2'=2] {'prow'}, dimensions={0} | all-to-all | bytes 393216 | tf_op jit(solution)/shard_map/all_to_all | solution.py:30
  461.0 0.5 broadcast.82
  461.5 1.1 reduce.9
  462.6 0.2 reshape.144
  462.9 0.1 reduce_sum.19
  462.9 0.0 copy-done.1
  463.0 0.6 sub.3
Async XLA Ops:
  13.3 188.1 %all-to-all-start = ((f32[16,3,80,512]{3,2,1,0:T(8,128)}), f32[16,3,80,512]{3,2,1,0:T(8,128)}, u32[]{:S(2)}, u32[]{:S(2)}) async-start(f32[16,3,80,512]{3,2,1,0:T(8,128)} %stack.2), calls=%async_computation | async-start | bytes 15728640 | tf_op jit(solution)/shard_map/all_to_all | solution.py:52
  24.5 276.1 %reduce-scatter.3.cloned.1.call-start = ((), (), s32[]{:S(2)}) async-start(), calls=%async_computation.5 | async-start | bytes 11796480 | tf_op jit(solution)/shard_map/reduce_scatter | solution.py:24
  273.4 119.1 %reduce-scatter.5.cloned.1.call-start = ((), (), s32[]{:S(2)}) async-start(), calls=%async_computation.6 | async-start | bytes 4423680 | tf_op jit(solution)/shard_map/reduce_scatter | solution.py:25
  393.6 2.7 copy-start
  441.2 21.7 %copy-start.1 = (f32[3,32,32]{2,1,0:T(8,128)S(1)}, f32[3,32,32]{2,1,0:T(8,128)}, u32[]{:S(2)}) copy-start(f32[3,32,32]{2,1,0:T(8,128)} %param.19) | copy-start | bytes 36868
Sparse Core Ops, SparseCore 0:
  273.5 27.1 reduce-scatter.2
  303.2 89.1 reduce-scatter.4
